TPU v7x, 32 devices: a whole 2x2x4 slice. The times are simulated.
32 devices in a mesh: fsdp: 8 (over y, x, core), blk: 4 (over z).
Axes of the slice: x: 2, y: 2, z: 4, core: 2. Of those that a mesh axis runs over, the one named last changes fastest.
Arguments:
- grad: bfloat16 [16, 768, 768], P(None, 'fsdp', 'blk'), may hold values from -16 to 16
- owner_slots: int32 [16], replicated, may hold values from 0 to 15, as said below
- stat_left: float32 [16, 768, 768], P('fsdp', None, 'blk'), may hold values from -6 to 6
- stat_right: float32 [16, 768, 768], P('fsdp', None, 'blk'), may hold values from -6 to 6
- basis_left: bfloat16 [16, 768, 768], P('fsdp'), may hold values from -1 to 1, as said below
- basis_right: bfloat16 [16, 768, 768], P('fsdp'), may hold values from -1 to 1, as said below
- moment: float32 [16, 768, 768], P('fsdp', None, 'blk'), may hold values from -3 to 3
- second: float32 [16, 768, 768], P('fsdp', None, 'blk'), may hold values from 0.01 to 0.1
Outputs:
- update: bfloat16 [16, 768, 768], P(None, 'fsdp', 'blk')
- new_left: float32 [16, 768, 768], P('fsdp', None, 'blk')
- new_right: float32 [16, 768, 768], P('fsdp', None, 'blk')
- new_moment: float32 [16, 768, 768], P('fsdp', None, 'blk')
- new_second: float32 [16, 768, 768], P('fsdp', None, 'blk')
- grad_rms: float32 [], replicated
Inputs may be any that keep to these rules, and one draw needn't show every extreme that they name: Each 768 x 768 block of basis_left is orthogonal up to bfloat16 rounding. Each 768 x 768 block of basis_right is orthogonal up to bfloat16 rounding. owner_slots names every block exactly once.
All inputs are finite; a program needn't handle non-finite values.
Results may differ from a plain program's by a relative error of at most 0.0058.
Values may be sent and summed in bfloat16 or wider, within the bound.
No kernel may reach another device: no remote copies, remote signals or barrier semaphores. Data moves between devices by JAX's collectives and lax.ppermute only.
A program may use at most 64 MiB of HBM per device.

v0:
```python
import jax
import jax.numpy as jnp
from jax import lax
from jax.sharding import PartitionSpec as P

BS = 768
clip_level = 0.5
stat_decay = 0.95
beta_one = 0.9
beta_two = 0.95
epsilon = 1e-08


def body(grad, owner_slots, stat_left, stat_right, basis_left, basis_right, moment, second):
    arranged = jnp.take(grad, owner_slots, axis=0)
    owned = lax.all_to_all(arranged, "fsdp", split_axis=0, concat_axis=1, tiled=True)
    width = owned.shape[2]
    first_col = lax.axis_index("blk") * width
    entries = grad.shape[0] * BS * BS
    partial_sum = jnp.sum(jnp.square(owned.astype(jnp.float32)))
    total = lax.psum(partial_sum, ("fsdp", "blk"))
    grad_rms = jnp.sqrt(total / entries)
    factor = jnp.minimum(1.0, clip_level / grad_rms)
    whole = lax.all_gather(owned, "blk", axis=2, tiled=True)
    own_rows = lax.dynamic_slice_in_dim(whole, first_col, width, 1)
    right_cols = lax.dynamic_slice_in_dim(basis_right, first_col, width, 2)
    outer_left = jnp.einsum("bij,bkj->bik", whole, own_rows, preferred_element_type=jnp.float32)
    outer_right = jnp.einsum("bji,bjk->bik", whole, owned, preferred_element_type=jnp.float32)
    new_left = stat_decay * stat_left + (1.0 - stat_decay) * (factor * factor) * outer_left
    new_right = stat_decay * stat_right + (1.0 - stat_decay) * (factor * factor) * outer_right
    turned = jnp.einsum(
        "bij,bjk->bik", whole, right_cols, preferred_element_type=jnp.float32
    ).astype(jnp.bfloat16)
    rotated = factor * jnp.einsum(
        "bji,bjk->bik", basis_left, turned, preferred_element_type=jnp.float32
    )
    new_moment = beta_one * moment + (1.0 - beta_one) * rotated
    new_second = beta_two * second + (1.0 - beta_two) * rotated * rotated
    scaled = (new_moment / (jnp.sqrt(new_second) + epsilon)).astype(jnp.bfloat16)
    back = jnp.einsum(
        "bij,bjk->bik", basis_left, scaled, preferred_element_type=jnp.float32
    ).astype(jnp.bfloat16)
    right_rows = lax.dynamic_slice_in_dim(basis_right, first_col, width, 1)
    summed = jnp.einsum(
        "bij,bkj->bik",
        lax.all_gather(back, "blk", axis=2, tiled=True),
        right_rows,
        preferred_element_type=jnp.float32,
    )
    stepped = summed.astype(jnp.bfloat16)
    returned = lax.all_to_all(stepped, "fsdp", split_axis=1, concat_axis=0, tiled=True)
    placed = jnp.zeros_like(returned).at[owner_slots].set(returned)
    return (placed, new_left, new_right, new_moment, new_second, grad_rms)


def solution(mesh):
    placed = (
        P(None, "fsdp", "blk"),
        P(),
        P("fsdp", None, "blk"),
        P("fsdp", None, "blk"),
        P("fsdp", None, None),
        P("fsdp", None, None),
        P("fsdp", None, "blk"),
        P("fsdp", None, "blk"),
    )
    return jax.shard_map(
        body,
        mesh=mesh,
        in_specs=placed,
        out_specs=(
            P(None, "fsdp", "blk"),
            P("fsdp", None, "blk"),
            P("fsdp", None, "blk"),
            P("fsdp", None, "blk"),
            P("fsdp", None, "blk"),
            P(),
        ),
        check_vma=False,
    )
```

profile of v0, /device:TPU:0, one launch (start us, length us, event | category | flops | bytes accessed | tf_op | source)
XLA Modules:
  0.0 176.2 jit_solution(13508039111027429911)
XLA Ops:
  7.2 0.0 copy-start
  7.2 0.0 all-gather.3.cloned.1.call-start
  7.2 0.8 compare_select_fusion
  8.0 0.7 compare_and_fusion
  8.7 1.7 gather_fusion
  10.4 0.1 broadcast_select_fusion
  10.6 17.6 %all_to_all.36 = bf16[16,96,192]{2,1,0:T(8,128)(2,1)} all-to-all(bf16[16,96,192]{2,1,0:T(8,128)(2,1)S(1)} %broadcast_select_fusion), channel_id=1, replica_groups=mesh['fsdp'=8,'blk'=4] {'fsdp'}, dimensions={0} | all-to-all | bytes 1179648 | tf_op jit(solution)/shard_map/all_to_all | solution.py:16
  28.2 1.6 copy.24
  29.8 1.5 all_to_all.29
  31.2 2.5 %copy.25 = bf16[2,768,192]{1,0,2:T(2,128)(2,1)} copy(bf16[2,768,192]{1,2,0:T(8,128)(2,1)} %all_to_all.29) | data formatting | bytes 1179648 | tf_op jit(solution)/shard_map/all_to_all | solution.py:16
  33.7 0.0 all-gather.3.cloned.1.call-update
  33.8 0.0 all-gather.5.cloned.1.call-start
  33.8 1.0 multiply_reduce_fusion
  34.8 43.4 %psum.7 = f32[]{:T(128)} all-reduce(f32[]{:T(128)} %multiply_reduce_fusion), channel_id=1, replica_groups=mesh['fsdp'=8,'blk'=4] {'fsdp','blk'}, use_global_device_ids=true, to_apply=%region_1.2 | all-reduce | flops 1 | bytes 8 | tf_op jit(solution)/shard_map/psum | solution.py:21
  79.0 5.3 %all-gather.3.cloned.1.call-done = bf16[2,768,768]{1,0,2:T(2,128)(2,1)} async-done(((bf16[2,768,192]{1,0,2:T(2,128)(2,1)}), bf16[2,768,768]{1,0,2:T(2,128)(2,1)}) %all-gather.3.cloned.1.call-update) | async-done | bytes 2359312 | tf_op jit(solution)/shard_map/all_gather | solution.py:24
  84.3 0.0 copy-done
  84.3 5.2 %fusion.25 = (f32[2,768,192]{1,2,0:T(8,128)S(1)}, f32[2,768,192]{1,2,0:T(8,128)}) fusion(f32[2,768,192]{1,2,0:T(8,128)} %param.15, f32[2,768,192]{1,2,0:T(8,128)} %param.14, bf16[2,768,768]{2,1,0:T(8,128)(2,1)S(1)} %copy-done, bf16[2,768,768]{1,0,2:T(2,128)(2,1)} %all-gather.3.cloned.1.call-done, bf16[2,768,768]{2,1,0:T(8,128)(2,1)} %param.13, ...), kind=kOutput, calls=%fused_computation.20 | convolution fusion | flops 908623872 | bytes 10223624 | tf_op jit(solution)/shard_map/bji,bjk->bik/dot_general | solution.py:34
  89.5 0.0 copy-start.3
  89.5 3.4 %fusion.22 = bf16[2,768,192]{1,2,0:T(8,128)(2,1)} fusion(bf16[2,768,768]{2,1,0:T(8,128)(2,1)S(1)} %copy-done, f32[2,768,192]{1,2,0:T(8,128)} %get-tuple-element.7, f32[2,768,192]{1,2,0:T(8,128)S(1)} %get-tuple-element.6), kind=kOutput, calls=%fused_computation.19 | convolution fusion | flops 454164480 | bytes 5308416 | tf_op jit(solution)/shard_map/bij,bjk->bik/dot_general | solution.py:40
  92.9 0.0 copy-done.3
  92.9 0.0 all-gather.5.cloned.1.call-update
  92.9 48.9 %all-gather.5.cloned.1.call-done = bf16[2,768,768]{1,2,0:T(8,128)(2,1)} async-done(((bf16[2,768,192]{1,2,0:T(8,128)(2,1)}), bf16[2,768,768]{1,2,0:T(8,128)(2,1)}) %all-gather.5.cloned.1.call-update) | async-done | bytes 2359312 | tf_op jit(solution)/shard_map/all_gather | solution.py:46
  141.9 2.5 %convolution_convert_fusion = bf16[2,768,192]{1,2,0:T(8,128)(2,1)S(1)} fusion(bf16[2,768,768]{1,2,0:T(8,128)(2,1)} %all-gather.5.cloned.1.call-done, bf16[2,768,768]{2,1,0:T(8,128)(2,1)} %param.13, s32[]{:T(128)S(6)} %select_n.17), kind=kOutput, calls=%fused_computation.17 | convolution fusion | flops 453279744 | bytes 3538948 | tf_op jit(solution)/shard_map/bij,bkj->bik/dot_general | solution.py:44
  144.4 1.8 %copy.28 = bf16[2,768,192]{2,0,1:T(2,128)(2,1)} copy(bf16[2,768,192]{1,2,0:T(8,128)(2,1)S(1)} %convolution_convert_fusion) | data formatting | bytes 1179648 | tf_op jit(solution)/shard_map/convert_element_type | solution.py:50
  146.1 3.7 %all-to-all-start.1 = ((bf16[2,768,192]{2,0,1:T(2,128)(2,1)}), bf16[2,768,192]{2,0,1:T(2,128)(2,1)S(1)}, u32[]{:S(2)}, u32[]{:S(2)}) async-start(bf16[2,768,192]{2,0,1:T(2,128)(2,1)} %copy.28), calls=%async_computation.1 | async-start | bytes 1572864 | tf_op jit(solution)/shard_map/all_to_all | solution.py:51
  149.8 0.0 copy-start.1
  149.8 4.3 %fusion.13 = f32[2,768,192]{1,2,0:T(8,128)} fusion(bf16[2,768,192]{1,2,0:T(8,128)(2,1)} %all_to_all.29, bf16[2,768,768]{1,0,2:T(2,128)(2,1)} %all-gather.3.cloned.1.call-done, f32[2,768,192]{1,2,0:T(8,128)} %param.11, f32[]{:T(128)S(6)} %mul.74), kind=kOutput, calls=%fused_computation.14 | convolution fusion | flops 453869568 | bytes 5308420 | tf_op jit(solution)/shard_map/bji,bjk->bik/dot_general | solution.py:28
  154.1 0.0 copy-done.1
  154.1 0.0 copy-start.4
  154.1 1.3 constant_dynamic-slice_fusion
  155.4 0.0 copy-done.4
  155.4 1.7 fusion.16
  157.1 5.3 %all-to-all-done.1 = bf16[2,768,192]{2,0,1:T(2,128)(2,1)S(1)} async-done(((bf16[2,768,192]{2,0,1:T(2,128)(2,1)}), bf16[2,768,192]{2,0,1:T(2,128)(2,1)S(1)}, u32[]{:S(2)}, u32[]{:S(2)}) %all-to-all-start.1) | async-done | bytes 589856 | tf_op jit(solution)/shard_map/all_to_all | solution.py:51
  162.4 0.0 copy-start.2
  162.4 0.9 copy-done.2
  163.2 1.3 copy.29
  164.5 1.0 broadcast_in_dim.16
  165.5 2.7 %scatter_fusion = bf16[16,96,192]{2,1,0:T(8,128)(2,1)} fusion(bf16[16,96,192]{2,1,0:T(8,128)(2,1)} %broadcast_in_dim.16, s32[16]{0:T(128)S(1)} %compare_select_fusion, bf16[16,96,192]{2,1,0:T(8,128)(2,1)S(1)} %bitcast.21), kind=kCustom, calls=%fused_computation.1 | custom fusion | bytes 1769536 | tf_op jit(solution)/shard_map/scatter | solution.py:52
  (1 shorter events, 0.0 us)
Async XLA Ops:
  7.2 77.1 %copy-start = (bf16[2,768,768]{2,1,0:T(8,128)(2,1)S(1)}, bf16[2,768,768]{2,1,0:T(8,128)(2,1)}, u32[]{:S(2)}) copy-start(bf16[2,768,768]{2,1,0:T(8,128)(2,1)} %param.12) | copy-start | bytes 7077892
  7.2 77.1 %all-gather.3.cloned.1.call-start = ((), (), s32[]{:S(2)}) async-start(), calls=%async_computation.2 | async-start | bytes 2949120 | tf_op jit(solution)/shard_map/all_gather | solution.py:24
  33.8 108.1 %all-gather.5.cloned.1.call-start = ((), (), s32[]{:S(2)}) async-start(), calls=%async_computation.3 | async-start | bytes 2949120 | tf_op jit(solution)/shard_map/all_gather | solution.py:46
  89.5 3.4 %copy-start.3 = (f32[2,768,192]{1,2,0:T(8,128)}, f32[2,768,192]{1,2,0:T(8,128)S(1)}, u32[]{:S(2)}) copy-start(f32[2,768,192]{1,2,0:T(8,128)S(1)} %get-tuple-element.6) | copy-start | bytes 3538948
  146.1 16.2 %all-to-all-start.1 = ((bf16[2,768,192]{2,0,1:T(2,128)(2,1)}), bf16[2,768,192]{2,0,1:T(2,128)(2,1)S(1)}, u32[]{:S(2)}, u32[]{:S(2)}) async-start(bf16[2,768,192]{2,0,1:T(2,128)(2,1)} %copy.28), calls=%async_computation.1 | async-start | bytes 1572864 | tf_op jit(solution)/shard_map/all_to_all | solution.py:51
  149.8 4.3 %copy-start.1 = (bf16[2,768,768]{1,0,2:T(2,128)(2,1)S(1)}, bf16[2,768,768]{1,0,2:T(2,128)(2,1)}, u32[]{:S(2)}) copy-start(bf16[2,768,768]{1,0,2:T(2,128)(2,1)} %all-gather.3.cloned.1.call-done) | copy-start | bytes 7077892
  154.1 1.3 copy-start.4
  162.4 0.9 copy-start.2
Sparse Core Ops, SparseCore 0:
  33.9 50.3 all-gather.2
  93.0 48.7 all-gather.4
where the time goes:
time: 177 us; the launch traced here: 176 us
  blocking collectives  61 us (34%)
  waiting for transfers between devices  59.6 us (34%)
  matrix products  17 us (10%)
  local copies, waits for them, and re-layouts  16.2 us (9%)
  between operations  16 us (9%)
  starting transfers between devices  3.73 us (2%)
  other arithmetic  2.62 us (1%)
    all_gather x1, waiting for transfers between devices, body(): lax.all_gather(back, 'blk', axis=2, tiled=True)  48.9 us
    psum x1, blocking collectives, body(): total = lax.psum(partial_sum, ('fsdp', 'blk'))  43.4 us
    all_to_all x1, blocking collectives, body(): lax.all_to_all(arranged, 'fsdp', split_axis=0, concat_axis=1, tiled=True)  17.6 us
    all_to_all x3, local copies, waits for them, and re-layouts, body(): lax.all_to_all(arranged, 'fsdp', split_axis=0, concat_axis=1, tiled=True)  5.5 us
    all_gather x1, waiting for transfers between devices, body(): whole = lax.all_gather(owned, 'blk', axis=2, tiled=True)  5.34 us
    all_to_all x1, waiting for transfers between devices, body(): lax.all_to_all(stepped, 'fsdp', split_axis=1, concat_axis=0, tiled=True)  5.27 us
    dot_general x1, matrix products, body(): jnp.einsum('bji,bjk->bik', basis_left, turned, preferred_element_type=jnp...  5.16 us
    dot_general x1, matrix products, body(): jnp.einsum('bji,bjk->bik', whole, owned, preferred_element_type=jnp.float32)  4.26 us
  transfers between devices with their start and end apart: 3, of which 3 were waited for; matrix products, arithmetic and copies ran while one was open for 5% of the time, Pallas kernels for 0%

commit v1 on v0

--- a/solution.py
+++ b/solution.py
@@ -41,12 +41,37 @@
         "bij,bjk->bik", basis_left, scaled, preferred_element_type=jnp.float32
     ).astype(jnp.bfloat16)
     right_rows = lax.dynamic_slice_in_dim(basis_right, first_col, width, 1)
+    devices, index, span = (lax.axis_size("blk"), lax.axis_index("blk"), back.shape[2])
+    right = [(i, (i + 1) % devices) for i in range(devices)]
+    behind = [(i, (i - 1) % devices) for i in range(devices)]
+    middle = devices // 2
+    from_left = from_right = back
     summed = jnp.einsum(
         "bij,bkj->bik",
-        lax.all_gather(back, "blk", axis=2, tiled=True),
-        right_rows,
+        back,
+        lax.dynamic_slice_in_dim(right_rows, index * span, back.shape[2], axis=2),
         preferred_element_type=jnp.float32,
     )
+    for step in range(1, middle + 1):
+        from_left = lax.ppermute(from_left, "blk", right)
+        if step < devices - middle:
+            from_right = lax.ppermute(from_right, "blk", behind)
+            summed = summed + jnp.einsum(
+                "bij,bkj->bik",
+                from_right,
+                lax.dynamic_slice_in_dim(
+                    right_rows, (index + step) % devices * span, from_right.shape[2], axis=2
+                ),
+                preferred_element_type=jnp.float32,
+            )
+        summed = summed + jnp.einsum(
+            "bij,bkj->bik",
+            from_left,
+            lax.dynamic_slice_in_dim(
+                right_rows, (index - step) % devices * span, from_left.shape[2], axis=2
+            ),
+            preferred_element_type=jnp.float32,
+        )
     stepped = summed.astype(jnp.bfloat16)
     returned = lax.all_to_all(stepped, "fsdp", split_axis=1, concat_axis=0, tiled=True)
     placed = jnp.zeros_like(returned).at[owner_slots].set(returned)

time: 177 us -> 169 us (0.955)
  waiting for transfers between devices: 59.6 us -> 46.8 us
  starting transfers between devices: 3.73 us -> 7.54 us
    all_gather x1 -> x0, waiting for transfers between devices: 48.9 us -> none  [body(): lax.all_gather(back, 'blk', axis=2, tiled=True)]
    ppermute x0 -> x3, waiting for transfers between devices: none -> 36.1 us  [the longest x2 26.6 us: body(): from_left = lax.ppermute(from_left, 'blk', right)]
    ppermute x0 -> x3, starting transfers between devices: none -> 3.83 us  [the longest x1 3.82 us: body(): from_right = lax.ppermute(from_right, 'blk', behind)]
  transfers between devices with their start and end apart: 3 -> 5, of which waited for: 3 -> 5; matrix products, arithmetic and copies ran while one was open for 5% -> 6% of each run, Pallas kernels for 0% -> 0%
where the time goes in v1:
time: 169 us; the launch traced here: 168 us
  blocking collectives  61.1 us (36%)
  waiting for transfers between devices  46.8 us (28%)
  matrix products  18.3 us (11%)
  local copies, waits for them, and re-layouts  16.2 us (10%)
  between operations  16 us (9%)
  starting transfers between devices  7.54 us (4%)
  other arithmetic  2.62 us (2%)
    psum x1, blocking collectives, body(): total = lax.psum(partial_sum, ('fsdp', 'blk'))  43.5 us
    ppermute x2, waiting for transfers between devices, body(): from_left = lax.ppermute(from_left, 'blk', right)  26.6 us
    all_to_all x1, blocking collectives, body(): lax.all_to_all(arranged, 'fsdp', split_axis=0, concat_axis=1, tiled=True)  17.6 us
    ppermute x1, waiting for transfers between devices, body(): from_right = lax.ppermute(from_right, 'blk', behind)  9.52 us
    all_to_all x3, local copies, waits for them, and re-layouts, body(): lax.all_to_all(arranged, 'fsdp', split_axis=0, concat_axis=1, tiled=True)  5.5 us
    dot_general x1, matrix products, body(): jnp.einsum('bji,bjk->bik', basis_left, turned, preferred_element_type=jnp...  5.5 us
    all_gather x1, waiting for transfers between devices, body(): whole = lax.all_gather(owned, 'blk', axis=2, tiled=True)  5.34 us
    all_to_all x1, waiting for transfers between devices, body(): lax.all_to_all(stepped, 'fsdp', split_axis=1, concat_axis=0, tiled=True)  5.27 us
  transfers between devices with their start and end apart: 5, of which 5 were waited for; matrix products, arithmetic and copies ran while one was open for 6% of the time, Pallas kernels for 0%

profile of v1, /device:TPU:0, one launch (start us, length us, event | category | flops | bytes accessed | tf_op | source)
XLA Modules:
  0.0 168.4 jit_solution(762076064847111056)
XLA Ops:
  7.2 0.0 copy-start
  7.2 0.0 all-gather.2.cloned.1.call-start
  7.2 0.8 compare_select_fusion
  8.0 0.7 compare_and_fusion
  8.7 1.7 %gather_fusion = bf16[16,96,192]{2,1,0:T(8,128)(2,1)S(1)} fusion(bf16[16,96,192]{2,1,0:T(8,128)(2,1)} %param.8, s32[1024]{0:T(1024)S(1)} %pad_clamp_fusion), kind=kCustom, calls=%fused_computation | custom fusion | bytes 1179712 | tf_op jit(solution)/shard_map/jit(_take)/gather | solution.py:15
  10.4 0.1 broadcast_select_fusion
  10.6 17.6 %all_to_all.36 = bf16[16,96,192]{2,1,0:T(8,128)(2,1)} all-to-all(bf16[16,96,192]{2,1,0:T(8,128)(2,1)S(1)} %broadcast_select_fusion), channel_id=1, replica_groups=mesh['fsdp'=8,'blk'=4] {'fsdp'}, dimensions={0} | all-to-all | bytes 1179648 | tf_op jit(solution)/shard_map/all_to_all | solution.py:16
  28.2 1.6 copy.24
  29.8 1.5 all_to_all.29
  31.2 2.5 %copy.25 = bf16[2,768,192]{1,0,2:T(2,128)(2,1)} copy(bf16[2,768,192]{1,2,0:T(8,128)(2,1)} %all_to_all.29) | data formatting | bytes 1179648 | tf_op jit(solution)/shard_map/all_to_all | solution.py:16
  33.7 0.0 all-gather.2.cloned.1.call-update
  33.8 1.0 multiply_reduce_fusion
  34.8 43.5 %psum.7 = f32[]{:T(128)} all-reduce(f32[]{:T(128)} %multiply_reduce_fusion), channel_id=1, replica_groups=mesh['fsdp'=8,'blk'=4] {'fsdp','blk'}, use_global_device_ids=true, to_apply=%region_1.2 | all-reduce | flops 1 | bytes 8 | tf_op jit(solution)/shard_map/psum | solution.py:21
  79.0 5.3 %all-gather.2.cloned.1.call-done = bf16[2,768,768]{1,0,2:T(2,128)(2,1)} async-done(((bf16[2,768,192]{1,0,2:T(2,128)(2,1)}), bf16[2,768,768]{1,0,2:T(2,128)(2,1)}) %all-gather.2.cloned.1.call-update) | async-done | bytes 2359312 | tf_op jit(solution)/shard_map/all_gather | solution.py:24
  84.3 0.0 copy-done
  84.3 5.5 %fusion.25 = (f32[2,768,192]{1,2,0:T(8,128)S(1)}, f32[2,768,192]{1,2,0:T(8,128)}) fusion(f32[2,768,192]{1,2,0:T(8,128)} %param.15, f32[2,768,192]{1,2,0:T(8,128)} %param.14, bf16[2,768,768]{2,1,0:T(8,128)(2,1)} %param.12, bf16[2,768,768]{1,0,2:T(2,128)(2,1)} %all-gather.2.cloned.1.call-done, bf16[2,768,768]{2,1,0:T(8,128)(2,1)S(1)} %copy-done, ...), kind=kOutput, calls=%fused_computation.22 | convolution fusion | flops 908623872 | bytes 10223624 | tf_op jit(solution)/shard_map/bji,bjk->bik/dot_general | solution.py:34
  89.8 0.0 copy-start.3
  89.8 4.2 %convolution_convert_fusion = bf16[2,192,768]{2,1,0:T(8,128)(2,1)} fusion(bf16[2,768,768]{2,1,0:T(8,128)(2,1)} %param.12, f32[2,768,192]{1,2,0:T(8,128)} %get-tuple-element.7, f32[2,768,192]{1,2,0:T(8,128)S(1)} %get-tuple-element.6), kind=kOutput, calls=%fused_computation.21 | convolution fusion | flops 454164480 | bytes 5308416 | tf_op jit(solution)/shard_map/bij,bjk->bik/dot_general | solution.py:40
  94.0 0.0 copy-done.3
  94.0 0.0 collective-permute-start.1
  94.0 3.8 %collective-permute-start = (bf16[2,768,192]{1,2,0:T(8,128)(2,1)}, bf16[2,768,192]{1,2,0:T(8,128)(2,1)S(1)}, u32[]{:S(2)}, u32[]{:S(2)}) collective-permute-start(bf16[2,768,192]{1,2,0:T(8,128)(2,1)} %bitcast.3), channel_id=1, source_target_pairs={{0,3},{1,0},{2,1},{3,2},{4,7},{5,4},{6,5},{7,6},{8,11},{9,8},{10,9... | collective-permute-start | bytes 1769480 | tf_op jit(solution)/shard_map/ppermute | solution.py:58
  97.8 1.5 fusion.33
  99.3 12.9 %collective-permute-done.1 = bf16[2,768,192]{1,2,0:T(8,128)(2,1)S(1)} collective-permute-done((bf16[2,768,192]{1,2,0:T(8,128)(2,1)}, bf16[2,768,192]{1,2,0:T(8,128)(2,1)S(1)}, u32[]{:S(2)}, u32[]{:S(2)}) %collective-permute-start.1) | collective-permute-done | bytes 589856 | tf_op jit(solution)/shard_map/ppermute | solution.py:56
  112.2 0.0 collective-permute-start.2
  112.2 9.5 %collective-permute-done = bf16[2,768,192]{1,2,0:T(8,128)(2,1)S(1)} collective-permute-done((bf16[2,768,192]{1,2,0:T(8,128)(2,1)}, bf16[2,768,192]{1,2,0:T(8,128)(2,1)S(1)}, u32[]{:S(2)}, u32[]{:S(2)}) %collective-permute-start) | collective-permute-done | bytes 589856 | tf_op jit(solution)/shard_map/ppermute | solution.py:58
  121.7 0.4 convolution_add_fusion.2
  122.1 0.4 convolution_add_fusion.1
  122.5 13.7 %collective-permute-done.2 = bf16[2,768,192]{1,2,0:T(8,128)(2,1)S(1)} collective-permute-done((bf16[2,768,192]{1,2,0:T(8,128)(2,1)S(1)}, bf16[2,768,192]{1,2,0:T(8,128)(2,1)S(1)}, u32[]{:S(2)}, u32[]{:S(2)}) %collective-permute-start.2) | collective-permute-done | bytes 589856 | tf_op jit(solution)/shard_map/ppermute | solution.py:56
  136.2 0.4 fusion.19
  136.6 1.8 %copy.28 = bf16[2,768,192]{2,0,1:T(2,128)(2,1)} copy(bf16[2,768,192]{1,2,0:T(8,128)(2,1)S(1)} %fusion.19) | data formatting | bytes 1179648 | tf_op jit(solution)/shard_map/convert_element_type | solution.py:75
  138.4 3.7 %all-to-all-start.1 = ((bf16[2,768,192]{2,0,1:T(2,128)(2,1)}), bf16[2,768,192]{2,0,1:T(2,128)(2,1)S(1)}, u32[]{:S(2)}, u32[]{:S(2)}) async-start(bf16[2,768,192]{2,0,1:T(2,128)(2,1)} %copy.28), calls=%async_computation.1 | async-start | bytes 1572864 | tf_op jit(solution)/shard_map/all_to_all | solution.py:76
  142.1 0.0 copy-start.1
  142.1 4.3 %fusion.13 = f32[2,768,192]{1,2,0:T(8,128)} fusion(bf16[2,768,192]{1,2,0:T(8,128)(2,1)} %all_to_all.29, bf16[2,768,768]{1,0,2:T(2,128)(2,1)} %all-gather.2.cloned.1.call-done, f32[2,768,192]{1,2,0:T(8,128)} %param.11, f32[]{:T(128)S(6)} %mul.87), kind=kOutput, calls=%fused_computation.17 | convolution fusion | flops 453869568 | bytes 5308420 | tf_op jit(solution)/shard_map/bji,bjk->bik/dot_general | solution.py:28
  146.3 0.0 copy-done.1
  146.3 0.0 copy-start.4
  146.3 1.3 constant_dynamic-slice_fusion
  147.6 0.0 copy-done.4
  147.7 1.7 %fusion.16 = f32[2,768,192]{1,2,0:T(8,128)} fusion(bf16[2,768,768]{1,0,2:T(2,128)(2,1)S(1)} %copy-done.1, f32[2,768,192]{1,2,0:T(8,128)S(1)} %copy-done.4, bf16[2,192,768]{1,0,2:T(2,128)(2,1)S(1)} %constant_dynamic-slice_fusion, f32[]{:T(128)S(6)} %mul.87), kind=kOutput, calls=%fused_computation.18 | convolution fusion | flops 453869568 | bytes 5308420 | tf_op jit(solution)/shard_map/bij,bkj->bik/dot_general | solution.py:27
  149.4 5.3 %all-to-all-done.1 = bf16[2,768,192]{2,0,1:T(2,128)(2,1)S(1)} async-done(((bf16[2,768,192]{2,0,1:T(2,128)(2,1)}), bf16[2,768,192]{2,0,1:T(2,128)(2,1)S(1)}, u32[]{:S(2)}, u32[]{:S(2)}) %all-to-all-start.1) | async-done | bytes 589856 | tf_op jit(solution)/shard_map/all_to_all | solution.py:76
  154.6 0.0 copy-start.2
  154.6 0.9 copy-done.2
  155.5 1.3 copy.29
  156.8 1.0 broadcast_in_dim.16
  157.7 2.7 %scatter_fusion = bf16[16,96,192]{2,1,0:T(8,128)(2,1)} fusion(bf16[16,96,192]{2,1,0:T(8,128)(2,1)} %broadcast_in_dim.16, s32[16]{0:T(128)S(1)} %compare_select_fusion, bf16[16,96,192]{2,1,0:T(8,128)(2,1)S(1)} %bitcast.22), kind=kCustom, calls=%fused_computation.1 | custom fusion | bytes 1769536 | tf_op jit(solution)/shard_map/scatter | solution.py:77
  (1 shorter events, 0.0 us)
Async XLA Ops:
  7.2 77.1 %copy-start = (bf16[2,768,768]{2,1,0:T(8,128)(2,1)S(1)}, bf16[2,768,768]{2,1,0:T(8,128)(2,1)}, u32[]{:S(2)}) copy-start(bf16[2,768,768]{2,1,0:T(8,128)(2,1)} %param.13) | copy-start | bytes 7077892
  7.2 77.1 %all-gather.2.cloned.1.call-start = ((), (), s32[]{:S(2)}) async-start(), calls=%async_computation.2 | async-start | bytes 2949120 | tf_op jit(solution)/shard_map/all_gather | solution.py:24
  89.8 4.2 %copy-start.3 = (f32[2,768,192]{1,2,0:T(8,128)}, f32[2,768,192]{1,2,0:T(8,128)S(1)}, u32[]{:S(2)}) copy-start(f32[2,768,192]{1,2,0:T(8,128)S(1)} %get-tuple-element.6) | copy-start | bytes 3538948
  94.0 18.2 %collective-permute-start.1 = (bf16[2,768,192]{1,2,0:T(8,128)(2,1)}, bf16[2,768,192]{1,2,0:T(8,128)(2,1)S(1)}, u32[]{:S(2)}, u32[]{:S(2)}) collective-permute-start(bf16[2,768,192]{1,2,0:T(8,128)(2,1)} %bitcast.3), channel_id=1, source_target_pairs={{0,1},{1,2},{2,3},{3,0},{4,5},{5,6},{6,7},{7,4},{8,9},{9,10},{10,1... | collective-permute-start | bytes 1769480 | tf_op jit(solution)/shard_map/ppermute | solution.py:56
  94.0 27.7 %collective-permute-start = (bf16[2,768,192]{1,2,0:T(8,128)(2,1)}, bf16[2,768,192]{1,2,0:T(8,128)(2,1)S(1)}, u32[]{:S(2)}, u32[]{:S(2)}) collective-permute-start(bf16[2,768,192]{1,2,0:T(8,128)(2,1)} %bitcast.3), channel_id=1, source_target_pairs={{0,3},{1,0},{2,1},{3,2},{4,7},{5,4},{6,5},{7,6},{8,11},{9,8},{10,9... | collective-permute-start | bytes 1769480 | tf_op jit(solution)/shard_map/ppermute | solution.py:58
  112.2 24.0 %collective-permute-start.2 = (bf16[2,768,192]{1,2,0:T(8,128)(2,1)S(1)}, bf16[2,768,192]{1,2,0:T(8,128)(2,1)S(1)}, u32[]{:S(2)}, u32[]{:S(2)}) collective-permute-start(bf16[2,768,192]{1,2,0:T(8,128)(2,1)S(1)} %collective-permute-done.1), channel_id=1, source_target_pairs={{0,1},{1,2},{2,3},{3,0},{4,5},{5,6},{6,7},{7,4},{8,9},{9,10},{10,1... | collective-permute-start | bytes 1769480 | tf_op jit(solution)/shard_map/ppermute | solution.py:56
  138.4 16.2 %all-to-all-start.1 = ((bf16[2,768,192]{2,0,1:T(2,128)(2,1)}), bf16[2,768,192]{2,0,1:T(2,128)(2,1)S(1)}, u32[]{:S(2)}, u32[]{:S(2)}) async-start(bf16[2,768,192]{2,0,1:T(2,128)(2,1)} %copy.28), calls=%async_computation.1 | async-start | bytes 1572864 | tf_op jit(solution)/shard_map/all_to_all | solution.py:76
  142.1 4.3 %copy-start.1 = (bf16[2,768,768]{1,0,2:T(2,128)(2,1)S(1)}, bf16[2,768,768]{1,0,2:T(2,128)(2,1)}, u32[]{:S(2)}) copy-start(bf16[2,768,768]{1,0,2:T(2,128)(2,1)} %all-gather.2.cloned.1.call-done) | copy-start | bytes 7077892
  146.3 1.3 copy-start.4
  154.6 0.9 copy-start.2
Sparse Core Ops, SparseCore 0:
  33.9 50.3 all-gather.1
